TPU v7x, 256 devices: a whole 4x4x8 slice. The times are simulated.
256 devices in a mesh: slab: 16 (over z_hi, x, core), chan: 16 (over y, z_lo).
Axes of the slice: x: 4, y: 4, z: 8 (z_hi: 2, z_lo: 4; z = z_hi * 4 + z_lo), core: 2. Of those that a mesh axis runs over, the one named last changes fastest.
Arguments:
- activations: bfloat16 [2, 128, 32, 16384], P(None, 'chan', 'slab'), may hold values from -6 to 6
- out_grad: bfloat16 [2, 256, 16, 4096], P(None, 'chan', 'slab'), may hold values from -6 to 6
- weights: bfloat16 [27, 128, 256], P(None, 'chan'), may hold values from -0.109375 to 0.109375
Outputs:
- input_grad: bfloat16 [2, 128, 32, 16384], P(None, 'chan', 'slab')
- weight_grad: float32 [27, 128, 256], P(None, 'chan', 'slab')
All inputs are finite; a program needn't handle non-finite values.
Results may differ from a plain program's by a relative error of at most 0.001.
Values may be sent and summed in bfloat16 or wider, within the bound.
A program may use at most 128 MiB of HBM per device.

v0:
```python
import math
import jax
import jax.numpy as jnp
from jax import lax
from jax.sharding import PartitionSpec as P

EDGE = 128


def from_behind(x, axis, by):
    count = lax.axis_size(axis)
    pairs = [(i, i + by) for i in range(count) if 0 <= i + by < count]
    return lax.ppermute(x, axis, pairs)


def flat_back(values, amount):
    zero_part = jnp.zeros(values.shape[:-1] + (amount,), values.dtype)
    return jnp.concatenate([zero_part, values[..., : values.shape[-1] - amount]], axis=-1)


def flat_ahead(values, amount):
    zero_part = jnp.zeros(values.shape[:-1] + (amount,), values.dtype)
    return jnp.concatenate([values[..., amount:], zero_part], axis=-1)


def column_index(length, half_edge):
    return lax.iota(jnp.int32, length) % half_edge


def tap_view(volume, row_tap, col_tap, half_edge):
    cells = half_edge * half_edge
    row_phase = 0 if row_tap == 1 else 1
    col_phase = 0 if col_tap == 1 else 1
    block = row_phase * 2 + col_phase
    picked = volume[..., block * cells : (block + 1) * cells]
    if row_tap == 0:
        picked = flat_back(picked, half_edge)
    if col_tap == 0:
        picked = flat_back(picked, 1)
        keep_mask = column_index(cells, half_edge) != 0
        picked = jnp.where(keep_mask, picked, jnp.zeros_like(picked))
    return picked


def assemble(fetch, half_edge, block_cells):
    last_column = column_index(block_cells, half_edge) == half_edge - 1
    rows_even = [fetch(1, col_tap) for col_tap in range(3)]
    rows_odd = [
        fetch(2, col_tap) + flat_ahead(fetch(0, col_tap), half_edge) for col_tap in range(3)
    ]
    phases = []
    for rows in (rows_even, rows_odd):
        phases.append(rows[1])
        moved = flat_ahead(rows[0], 1)
        phases.append(rows[2] + jnp.where(last_column, jnp.zeros_like(moved), moved))
    return jnp.concatenate(phases, axis=-1)


def body(activations, out_grad, weights):
    samples, chan_local, planes, plane_cells = activations.shape
    half_edge = EDGE // 2
    cells = half_edge * half_edge
    out_planes = planes // 2
    phased = activations.reshape(samples, chan_local, out_planes, 2, plane_cells)
    even_planes = phased[:, :, :, 0]
    odd_planes = phased[:, :, :, 1]
    previous = from_behind(odd_planes[:, :, out_planes - 1], "slab", 1)
    odd_before = jnp.concatenate([previous[:, :, None], odd_planes[:, :, : out_planes - 1]], axis=2)
    depth_views = (odd_before, even_planes, odd_planes)
    following = from_behind(out_grad[:, :, 0], "slab", -1)
    source = jnp.concatenate([out_grad, following[:, :, None]], axis=2)
    signal = lax.all_gather(source, "chan", axis=1, tiled=True)
    own_planes = signal[:, :, :out_planes]
    pieces = []
    for depth_tap in range(3):
        stacked = jnp.stack(
            [
                tap_view(depth_views[depth_tap], row_tap, col_tap, half_edge)
                for row_tap in range(3)
                for col_tap in range(3)
            ]
        )
        pieces.append(
            jnp.einsum("tbcdp,bkdp->tck", stacked, own_planes, preferred_element_type=jnp.float32)
        )
    local_grad = jnp.concatenate(pieces, axis=0)
    total_cells = samples * out_planes * lax.axis_size("slab") * half_edge * half_edge
    weight_grad = lax.psum_scatter(local_grad, "slab", scatter_dimension=2, tiled=True) * (
        1.0 / math.sqrt(total_cells)
    )
    first_block = signal[:, :, 1:]
    blocks = (first_block, own_planes, own_planes)
    folded = []
    for depth_tap in range(3):
        groups = jnp.einsum(
            "tck,bkdp->tbcdp",
            weights[9 * depth_tap : 9 * depth_tap + 9],
            blocks[depth_tap],
            preferred_element_type=jnp.float32,
        )

        def fetch(row_tap, col_tap, groups=groups):
            return groups[3 * row_tap + col_tap]

        folded.append(assemble(fetch, half_edge, cells))
    shifted = folded[0]
    odd_out = folded[2] + shifted
    chan_rows = folded[1].shape[1]
    kept_cells = 4 * cells
    local_grad_in = (
        jnp.stack([folded[1], odd_out], axis=3)
        .reshape(samples, chan_rows, planes, kept_cells)
        .astype(jnp.bfloat16)
    )
    return (local_grad_in, weight_grad)


def solution(mesh):
    placed = (P(None, "chan", "slab", None), P(None, "chan", "slab", None), P(None, "chan", None))
    return jax.shard_map(
        body,
        mesh=mesh,
        in_specs=placed,
        out_specs=(P(None, "chan", "slab", None), P(None, "chan", "slab")),
        check_vma=False,
    )
```

profile of v0, /device:TPU:8, one launch (start us, length us, event | category | flops | bytes accessed | tf_op | source)
XLA Modules:
  0.0 308.4 jit_solution(10184188523158755231)
XLA Ops:
  7.2 1.3 collective-permute-start
  8.5 1.8 copy.115
  10.4 3.1 collective-permute-start.1
  14.3 0.8 bitcast_dynamic-update-slice_fusion.10
  15.1 0.9 bitcast_dynamic-update-slice_fusion.8
  16.1 0.8 bitcast_dynamic-update-slice_fusion.7
  16.8 0.8 pad_maximum_fusion.1
  17.8 0.7 bitcast_dynamic-update-slice_fusion.6
  18.5 0.7 fusion.56
  19.2 0.7 fusion.55
  19.9 0.8 bitcast_dynamic-update-slice_fusion.5
  20.6 0.7 fusion.58
  21.3 0.7 fusion.54
  21.9 0.7 fusion.53
  23.5 184.6 %all-gather.2.cloned.1.call-done = bf16[2,256,2,4096]{3,1,0,2:T(8,128)(2,1)} async-done(((bf16[2,16,2,4096]{3,1,0,2:T(8,128)(2,1)}), bf16[2,256,2,4096]{3,1,0,2:T(8,128)(2,1)}) %all-gather.2.cloned.1.call-update) | async-done | bytes 8388624 | tf_op jit(solution)/shard_map/all_gather | solution.py:72
  208.1 3.1 %convolution_bitcast_fusion = f32[9,2,8,1,4096]{4,0,2,1,3:T(8,128)S(1)} fusion(bf16[2,256,2,4096]{3,1,0,2:T(8,128)(2,1)} %all-gather.2.cloned.1.call-done, bf16[9,8,256]{2,1,0:T(8,128)(2,1)S(1)} %get-tuple-element.47), kind=kOutput, calls=%fused_computation | convolution fusion | flops 301989888 | bytes 6590464 | tf_op jit(solution)/shard_map/tck,bkdp->tbcdp/dot_general | solution.py:95
  211.2 0.3 slice.336
  211.5 1.0 fusion.72
  212.5 1.5 copy-done.6
  214.1 1.4 fusion.21
  215.5 1.4 fusion.16
  216.9 1.4 fusion.26
  218.3 1.4 copy.59
  219.8 3.0 convolution_bitcast_fusion.2
  223.1 0.1 slice.359
  223.2 0.1 slice.356
  223.3 0.1 slice.353
  223.5 0.2 copy.114
  223.6 0.2 squeeze.88
  223.8 0.2 copy.117
  224.1 0.6 slice.345
  224.7 0.6 slice.342
  225.3 0.6 slice.348
  225.9 3.0 convolution_bitcast_fusion.1
  229.2 0.1 slice.374
  229.4 0.1 slice.371
  229.6 0.2 pad_add_fusion.1
  229.9 0.2 pad_add_fusion
  230.1 0.5 fusion.42
  230.5 0.2 copy.45
  230.8 1.4 pad_add_fusion.2
  232.1 3.2 %fusion.52 = (bf16[2,8,1,4096]{3,2,1,0:T(2,128)(2,1)S(1)}, bf16[2,8,1,4096]{3,2,1,0:T(2,128)(2,1)S(1)}) fusion(f32[9,2,8,1,4096]{4,0,2,1,3:T(8,128)} %copy-done, f32[2,8,1,4032]{3,2,1,0:T(1,128)S(1)} %slice.342, f32[2,8,1,4095]{3,2,1,0:T(1,128)S(1)} %pad_add_fusion.2, pred[4096]{0:T(1024)(128)(4,1)S(1)} %fusion.70, f32[2,8,1,4032]{3,2,1,0:T(1,128)S(1)} %slice.345), kind=kLoop, calls=%fused_computation.84 | loop fusion | flops 393216 | bytes 1568704 | tf_op jit(solution)/shard_map/convert.5
  235.4 1.1 pad_maximum_fusion
  236.5 0.6 copy.116
  237.3 2.1 copy.60
  239.4 60.7 %reduce-scatter.2.cloned.1.call-done = f32[27,8,16]{0,1,2:T(8,128)} async-done(((f32[27,8,256]{0,1,2:T(8,128)}), f32[27,8,16]{0,1,2:T(8,128)}) %reduce-scatter.2.cloned.1.call-update) | async-done | bytes 13840 | tf_op jit(solution)/shard_map/reduce_scatter | solution.py:88
  300.1 0.8 broadcast_multiply_fusion
  300.9 0.6 copy.61
  (57 shorter events, 2.7 us)
Async XLA Ops:
  7.2 200.9 %all-gather.2.cloned.1.call-start = ((), (), s32[]{:S(2)}) async-start(), calls=%async_computation.1 | async-start | bytes 8912896 | tf_op jit(solution)/shard_map/all_gather | solution.py:72
  7.2 9.6 %collective-permute-start = (bf16[2,16,4096]{2,1,0:T(8,128)(2,1)}, bf16[2,16,4096]{2,1,0:T(8,128)(2,1)S(1)}, u32[]{:S(2)}, u32[]{:S(2)}) collective-permute-start(bf16[2,16,4096]{2,1,0:T(8,128)(2,1)} %bitcast.307), channel_id=1, source_target_pairs={{16,0},{32,16},{48,32},{64,48},{80,64},{96,80},{112,96},{128,112},... | collective-permute-start | bytes 786440 | tf_op jit(solution)/shard_map/ppermute | solution.py:13
  10.4 12.3 %collective-permute-start.1 = (bf16[2,8,16384]{2,1,0:T(8,128)(2,1)S(1)}, bf16[2,8,16384]{2,1,0:T(8,128)(2,1)S(1)}, u32[]{:S(2)}, u32[]{:S(2)}) collective-permute-start(bf16[2,8,16384]{2,1,0:T(8,128)(2,1)S(1)} %get-tuple-element.32), channel_id=1, source_target_pairs={{0,16},{16,32},{32,48},{48,64},{64,80},{80,96},{96,112},{112,128},... | collective-permute-start | bytes 1572872 | tf_op jit(solution)/shard_map/ppermute | solution.py:13
  13.9 2.9 copy-start.1
  15.1 1.7 copy-start.3
  17.7 5.0 %copy-start.2 = (bf16[27,8,256]{2,1,0:T(8,128)(2,1)S(1)}, bf16[27,8,256]{2,1,0:T(8,128)(2,1)}, u32[]{:S(2)}) copy-start(bf16[27,8,256]{2,1,0:T(8,128)(2,1)} %param.5) | copy-start | bytes 331780
  17.7 282.4 %reduce-scatter.2.cloned.1.call-start = ((), (), s32[]{:S(2)}) async-start(), calls=%async_computation.2 | async-start | bytes 1114112 | tf_op jit(solution)/shard_map/reduce_scatter | solution.py:88
  208.1 6.0 %copy-start.6 = (bf16[2,256,2,4096]{3,1,0,2:T(8,128)(2,1)S(1)}, bf16[2,256,2,4096]{3,1,0,2:T(8,128)(2,1)}, u32[]{:S(2)}) copy-start(bf16[2,256,2,4096]{3,1,0,2:T(8,128)(2,1)} %all-gather.2.cloned.1.call-done) | copy-start | bytes 25165828
  211.2 4.3 %copy-start = (f32[9,2,8,1,4096]{4,0,2,1,3:T(8,128)}, f32[9,2,8,1,4096]{4,0,2,1,3:T(8,128)S(1)}, u32[]{:S(2)}) copy-start(f32[9,2,8,1,4096]{4,0,2,1,3:T(8,128)S(1)} %convolution_bitcast_fusion) | copy-start | bytes 7077892
  214.1 1.4 copy-start.5
  215.5 1.4 copy-start.4
Sparse Core Ops, SparseCore 0:
  17.8 190.2 all-gather.1
  219.9 80.1 reduce-scatter.1
where the time goes:
time: 309 us; the launch traced here: 308 us
  waiting for transfers between devices  245 us (79%)
  local copies, waits for them, and re-layouts  19.5 us (6%)
  between operations  14.5 us (5%)
  matrix products  13.3 us (4%)
  other arithmetic  11.4 us (4%)
  starting transfers between devices  4.44 us (1%)
    all_gather x1, waiting for transfers between devices, body(): signal = lax.all_gather(source, 'chan', axis=1, tiled=True)  185 us
    reduce_scatter x1, waiting for transfers between devices, body(): lax.psum_scatter(local_grad, 'slab', scatter_dimension=2, tiled=True)  60.7 us
    unnamed x35, local copies, waits for them, and re-layouts  11.8 us
    dot_general x3, matrix products, body(): jnp.einsum('tck,bkdp->tbcdp', weights[9 * depth_tap:9 * depth_tap + 9], b...  9.15 us
  transfers between devices with their start and end apart: 4, of which 2 were waited for; matrix products, arithmetic and copies ran while one was open for 10% of the time, Pallas kernels for 0%

commit v1 on v0

--- a/solution.py
+++ b/solution.py
@@ -69,7 +69,9 @@
     depth_views = (odd_before, even_planes, odd_planes)
     following = from_behind(out_grad[:, :, 0], "slab", -1)
     source = jnp.concatenate([out_grad, following[:, :, None]], axis=2)
-    signal = lax.all_gather(source, "chan", axis=1, tiled=True)
+    signal = jnp.concatenate(
+        lax.all_to_all(jnp.stack([source] * lax.axis_size("chan")), "chan", 0, 0), axis=1
+    )
     own_planes = signal[:, :, :out_planes]
     pieces = []
     for depth_tap in range(3):

time: 309 us -> 326 us (1.055)
  local copies, waits for them, and re-layouts: 19.5 us -> 31.9 us
  starting transfers between devices: 4.44 us -> 13.6 us
    all_gather x1 -> x0, waiting for transfers between devices: 185 us -> none  [body(): signal = lax.all_gather(source, 'chan', axis=1, tiled=True)]
    all_to_all x0 -> x1, waiting for transfers between devices: none -> 180 us  [body(): lax.all_to_all(jnp.stack([source] * lax.axis_size('chan')), 'chan', 0, 0)]
    all_to_all x0 -> x1, starting transfers between devices: none -> 8.99 us  [body(): lax.all_to_all(jnp.stack([source] * lax.axis_size('chan')), 'chan', 0, 0)]
    reshape x0 -> x1, local copies, waits for them, and re-layouts: none -> 7.71 us  [body(): jnp.concatenate(lax.all_to_all(jnp.stack([source] * lax.axis_size('chan')...]
    another operation x1 -> x2, local copies, waits for them, and re-layouts: 0.25 us -> 4.51 us  [the longest x1 4.26 us: body(): jnp.stack([source] * lax.axis_size('chan'))]
  transfers between devices with their start and end apart: 4 -> 4, of which waited for: 2 -> 2; matrix products, arithmetic and copies ran while one was open for 10% -> 11% of each run, Pallas kernels for 0% -> 0%
where the time goes in v1:
time: 326 us
  waiting for transfers between devices  242 us (74%)
  local copies, waits for them, and re-layouts  31.9 us (10%)
  between operations  14.5 us (4%)
  starting transfers between devices  13.6 us (4%)
  matrix products  13.4 us (4%)
  other arithmetic  10.7 us (3%)
    all_to_all x1, waiting for transfers between devices, body(): lax.all_to_all(jnp.stack([source] * lax.axis_size('chan')), 'chan', 0, 0)  180 us
    reduce_scatter x1, waiting for transfers between devices, body(): lax.psum_scatter(local_grad, 'slab', scatter_dimension=2, tiled=True)  61.1 us
    unnamed x35, local copies, waits for them, and re-layouts  11.8 us
    dot_general x3, matrix products, body(): jnp.einsum('tck,bkdp->tbcdp', weights[9 * depth_tap:9 * depth_tap + 9], b...  9.18 us
    all_to_all x1, starting transfers between devices, body(): lax.all_to_all(jnp.stack([source] * lax.axis_size('chan')), 'chan', 0, 0)  8.99 us
    reshape x1, local copies, waits for them, and re-layouts, body(): jnp.concatenate(lax.all_to_all(jnp.stack([source] * lax.axis_size('chan')...  7.71 us
  transfers between devices with their start and end apart: 4, of which 2 were waited for; matrix products, arithmetic and copies ran while one was open for 11% of the time, Pallas kernels for 0%

profile of v1, /device:TPU:8, one launch (start us, length us, event | category | flops | bytes accessed | tf_op | source)
XLA Modules:
  0.0 325.7 jit_solution(4392997318855685547)
XLA Ops:
  7.2 1.3 collective-permute-start
  8.5 1.8 copy.116
  10.4 3.1 collective-permute-start.1
  14.3 0.8 bitcast_dynamic-update-slice_fusion.10
  15.1 0.9 bitcast_dynamic-update-slice_fusion.8
  16.0 0.8 bitcast_dynamic-update-slice_fusion.7
  16.9 4.3 %stack.118 = bf16[16,2,16,2,4096]{4,2,1,3,0:T(8,128)(2,1)} broadcast(bf16[2,16,2,4096]{3,1,0,2:T(8,128)(2,1)S(1)} %copy.33), dimensions={1,2,3,4} | broadcast | bytes 8912896 | tf_op jit(solution)/shard_map/stack | solution.py:73
  21.1 9.0 %all-to-all-start = ((bf16[16,2,16,2,4096]{4,2,1,3,0:T(8,128)(2,1)}), bf16[16,2,16,2,4096]{4,2,1,3,0:T(8,128)(2,1)}, u32[]{:S(2)}, u32[]{:S(2)}) async-start(bf16[16,2,16,2,4096]{4,2,1,3,0:T(8,128)(2,1)} %stack.118), calls=%async_computation | async-start | bytes 16777216 | tf_op jit(solution)/shard_map/all_to_all | solution.py:73
  30.1 0.2 reduce-scatter.2.cloned.1.call-start
  30.4 0.8 bitcast_dynamic-update-slice_fusion.6
  31.1 0.7 fusion.56
  31.8 0.7 fusion.55
  32.4 0.8 bitcast_dynamic-update-slice_fusion.5
  33.2 0.6 fusion.54
  33.8 0.7 fusion.58
  34.5 0.7 fusion.53
  36.1 180.5 %all-to-all-done = bf16[16,2,16,2,4096]{4,2,1,3,0:T(8,128)(2,1)} async-done(((bf16[16,2,16,2,4096]{4,2,1,3,0:T(8,128)(2,1)}), bf16[16,2,16,2,4096]{4,2,1,3,0:T(8,128)(2,1)}, u32[]{:S(2)}, u32[]{:S(2)}) %all-to-all-start) | async-done | bytes 8388640 | tf_op jit(solution)/shard_map/all_to_all | solution.py:73
  216.5 7.7 %copy.34 = bf16[2,16,16,2,4096]{4,2,1,0,3:T(8,128)(2,1)} copy(bf16[2,16,16,2,4096]{4,2,0,3,1:T(8,128)(2,1)} %bitcast.2) | data formatting | bytes 16777216 | tf_op jit(solution)/shard_map/reshape | solution.py:72
  224.2 3.1 convolution_bitcast_fusion
  227.3 1.5 fusion.72
  228.8 0.3 slice.336
  229.1 1.1 copy-done
  230.2 0.5 copy-done.5
  230.8 1.4 fusion.26
  232.2 1.4 fusion.16
  233.6 1.4 fusion.21
  235.0 1.4 copy.60
  236.4 3.0 convolution_bitcast_fusion.2
  239.7 3.0 convolution_bitcast_fusion.1
  243.0 0.1 slice.353
  243.9 0.2 copy.118
  244.2 0.2 pad_add_fusion.1
  244.4 0.2 pad_add_fusion
  244.6 0.5 fusion.42
  245.1 0.2 copy.46
  245.3 0.6 slice.348
  246.0 0.6 slice.342
  246.6 0.6 slice.345
  247.2 0.1 copy.115
  247.3 0.2 squeeze.88
  247.5 1.4 pad_add_fusion.2
  248.9 3.3 %fusion.52 = (bf16[2,8,1,4096]{3,2,1,0:T(2,128)(2,1)S(1)}, bf16[2,8,1,4096]{3,2,1,0:T(2,128)(2,1)S(1)}) fusion(f32[9,2,8,1,4096]{4,0,2,1,3:T(8,128)} %copy-done.1, f32[2,8,1,4032]{3,2,1,0:T(1,128)S(1)} %slice.342, f32[2,8,1,4095]{3,2,1,0:T(1,128)S(1)} %pad_add_fusion.2, pred[4096]{0:T(1024)(128)(4,1)S(1)} %fusion.70, f32[2,8,1,4032]{3,2,1,0:T(1,128)S(1)} %slice.345), kind=kLoop, calls=%fused_computation.84 | loop fusion | flops 393216 | bytes 1568704 | tf_op jit(solution)/shard_map/convert.5
  252.2 1.1 pad_maximum_fusion
  253.3 0.6 copy.117
  254.1 2.1 copy.61
  256.2 61.1 %reduce-scatter.2.cloned.1.call-done = f32[27,8,16]{0,1,2:T(8,128)} async-done(((f32[27,8,256]{0,1,2:T(8,128)}), f32[27,8,16]{0,1,2:T(8,128)}) %reduce-scatter.2.cloned.1.call-update) | async-done | bytes 13840 | tf_op jit(solution)/shard_map/reduce_scatter | solution.py:90
  317.3 0.8 broadcast_multiply_fusion
  318.2 0.6 copy.62
  (59 shorter events, 3.2 us)
Async XLA Ops:
  7.2 9.6 %collective-permute-start = (bf16[2,16,4096]{2,1,0:T(8,128)(2,1)}, bf16[2,16,4096]{2,1,0:T(8,128)(2,1)S(1)}, u32[]{:S(2)}, u32[]{:S(2)}) collective-permute-start(bf16[2,16,4096]{2,1,0:T(8,128)(2,1)} %bitcast.314), channel_id=1, source_target_pairs={{16,0},{32,16},{48,32},{64,48},{80,64},{96,80},{112,96},{128,112},... | collective-permute-start | bytes 786440 | tf_op jit(solution)/shard_map/ppermute | solution.py:13
  10.4 24.9 %collective-permute-start.1 = (bf16[2,8,16384]{2,1,0:T(8,128)(2,1)S(1)}, bf16[2,8,16384]{2,1,0:T(8,128)(2,1)S(1)}, u32[]{:S(2)}, u32[]{:S(2)}) collective-permute-start(bf16[2,8,16384]{2,1,0:T(8,128)(2,1)S(1)} %get-tuple-element.32), channel_id=1, source_target_pairs={{0,16},{16,32},{32,48},{48,64},{64,80},{80,96},{96,112},{112,128},... | collective-permute-start | bytes 1572872 | tf_op jit(solution)/shard_map/ppermute | solution.py:13
  13.9 2.8 copy-start.2
  15.1 1.7 copy-start.4
  21.1 195.4 %all-to-all-start = ((bf16[16,2,16,2,4096]{4,2,1,3,0:T(8,128)(2,1)}), bf16[16,2,16,2,4096]{4,2,1,3,0:T(8,128)(2,1)}, u32[]{:S(2)}, u32[]{:S(2)}) async-start(bf16[16,2,16,2,4096]{4,2,1,3,0:T(8,128)(2,1)} %stack.118), calls=%async_computation | async-start | bytes 16777216 | tf_op jit(solution)/shard_map/all_to_all | solution.py:73
  30.1 5.1 %copy-start.3 = (bf16[27,8,256]{2,1,0:T(8,128)(2,1)S(1)}, bf16[27,8,256]{2,1,0:T(8,128)(2,1)}, u32[]{:S(2)}) copy-start(bf16[27,8,256]{2,1,0:T(8,128)(2,1)} %param.5) | copy-start | bytes 331780
  30.1 287.2 %reduce-scatter.2.cloned.1.call-start = ((), (), s32[]{:S(2)}) async-start(), calls=%async_computation.2 | async-start | bytes 1114112 | tf_op jit(solution)/shard_map/reduce_scatter | solution.py:90
  224.2 6.0 %copy-start = (bf16[2,16,16,2,4096]{4,2,1,0,3:T(8,128)(2,1)S(1)}, bf16[2,16,16,2,4096]{4,2,1,0,3:T(8,128)(2,1)}, u32[]{:S(2)}) copy-start(bf16[2,16,16,2,4096]{4,2,1,0,3:T(8,128)(2,1)} %copy.34) | copy-start | bytes 25165828
  227.3 4.8 %copy-start.1 = (f32[9,2,8,1,4096]{4,0,2,1,3:T(8,128)}, f32[9,2,8,1,4096]{4,0,2,1,3:T(8,128)S(1)}, u32[]{:S(2)}) copy-start(f32[9,2,8,1,4096]{4,0,2,1,3:T(8,128)S(1)} %convolution_bitcast_fusion) | copy-start | bytes 7077892
  227.3 3.4 %copy-start.5 = (bf16[9,2,8,1,4096]{4,2,1,3,0:T(8,128)(2,1)S(1)}, bf16[9,2,8,1,4096]{4,2,1,3,0:T(8,128)(2,1)}, u32[]{:S(2)}) copy-start(bf16[9,2,8,1,4096]{4,2,1,3,0:T(8,128)(2,1)} %get-tuple-element.60) | copy-start | bytes 3538948
  230.8 1.4 copy-start.6
Sparse Core Ops, SparseCore 0:
  236.6 80.7 reduce-scatter.1
